TPU v7x, 32 devices: a whole 2x2x4 slice. The times are simulated.
32 devices in a mesh: section: 2 (over core), dp: 4 (over y, x), ctx: 4 (over z).
Axes of the slice: x: 2, y: 2, z: 4, core: 2. Of those that a mesh axis runs over, the one named last changes fastest.
Arguments:
- tokens: bfloat16 [2, 8, 1024, 768], P(None, 'dp', 'ctx'), may hold values from -6 to 6
- upstream: bfloat16 [2, 8, 1024, 768], P(None, 'dp', 'ctx'), may hold values from -6 to 6
- lengths: int32 [2, 8], P(None, 'dp'), may hold values from 512 to 1024, as said below
- w_qkv: float32 [2, 768, 2304], P('section', ('dp', 'ctx')), may hold values from -0.21875 to 0.21875
- w_out: float32 [2, 768, 768], P('section', ('dp', 'ctx')), may hold values from -4 to 4
- w_in: float32 [2, 768, 3072], P('section', ('dp', 'ctx')), may hold values from -0.21875 to 0.21875
- w_back: float32 [2, 3072, 768], P('section', ('dp', 'ctx')), may hold values from -0.109375 to 0.109375
- gain_attn: float32 [2, 768], P('section', ('dp', 'ctx')), may hold values from 0.1 to 1.9
- gain_ffn: float32 [2, 768], P('section', ('dp', 'ctx')), may hold values from 0.1 to 1.9
Outputs:
- acts: float32 [2, 2, 8, 1024, 768], P('section', None, 'dp', 'ctx')
- grads: float32 [2, 2, 8, 1024, 768], P('section', None, 'dp', 'ctx')
- grad_qkv: float32 [2, 768, 2304], P('section', ('dp', 'ctx'))
- grad_out: float32 [2, 768, 768], P('section', ('dp', 'ctx'))
- grad_in: float32 [2, 768, 3072], P('section', ('dp', 'ctx'))
- grad_back: float32 [2, 3072, 768], P('section', ('dp', 'ctx'))
- grad_gain_attn: float32 [2, 768], P('section', ('dp', 'ctx'))
- grad_gain_ffn: float32 [2, 768], P('section', ('dp', 'ctx'))
Inputs may be any that keep to these rules, and one draw needn't show every extreme that they name: `lengths`: the number of real codons of each sequence, from 512 to 1024; some sequence has exactly 1024 and some exactly 512.
All inputs are finite; a program needn't handle non-finite values.
Results may differ from a plain program's by a relative error of at most 0.038.
Values may be sent and summed in bfloat16 or wider, within the bound.
No kernel may reach another device: no remote copies, remote signals or barrier semaphores. Data moves between devices by JAX's collectives and lax.ppermute only.
A program may use at most 320 MiB of HBM per device.

v0:
```python
from functools import partial
import jax
import jax.numpy as jnp
from jax import lax
from jax.sharding import PartitionSpec as P

HD = 64


def passed_along(value, axis, steps):
    count = lax.axis_size(axis)
    leading, last = (max(0, -steps), min(count, count - steps))
    return lax.ppermute(value, axis, [(source, source + steps) for source in range(leading, last)])


def tables(positions):
    half_width = HD // 2
    frequency = jnp.power(10000.0, -(jnp.arange(half_width).astype(jnp.float32) * 2.0) / HD)
    angles = positions[:, None] * frequency[None, :]
    angles = jnp.concatenate([angles, angles], axis=1)
    return (jnp.cos(angles)[:, None, :], jnp.sin(angles)[:, None, :])


def rotate(tensor, cosine_tab, sine_tab):
    half_width = tensor.shape[-1] // 2
    turned = jnp.concatenate([-tensor[..., half_width:], tensor[..., :half_width]], axis=-1)
    return tensor * cosine_tab + turned * sine_tab


def layer_norm(residual_state, gain_vec):
    centred = residual_state - jnp.mean(residual_state, axis=-1, keepdims=True)
    spread = jnp.mean(centred * centred, axis=-1, keepdims=True)
    return centred * lax.rsqrt(spread + 1e-05) * gain_vec


def contract_rows(left_op, right_op):
    return lax.dot_general(
        left_op, right_op, (((0,), (0,)), ((), ())), preferred_element_type=jnp.float32
    )


def contract_cols(left_op, right_op):
    return lax.dot_general(
        left_op, right_op, (((1,), (1,)), ((), ())), preferred_element_type=jnp.float32
    )


def store(buffer, new_value, position, in_range):
    previous = lax.dynamic_index_in_dim(buffer, position, 0, keepdims=False)
    return lax.dynamic_update_index_in_dim(
        buffer, jnp.where(in_range, new_value, previous), position, 0
    )


def split_heads(tensor):
    return tensor.reshape(tensor.shape[0], tensor.shape[1], tensor.shape[2] // HD, HD)


def masked_scores(query, key_all, key_mask):
    scores = jnp.einsum(
        "sqhd,skhd->shqk",
        split_heads(query),
        split_heads(key_all),
        preferred_element_type=jnp.float32,
    )
    return jnp.where(key_mask[:, None, None, :], scores, -1e30)


def attention_forward(query, key_all, value_all, key_mask):
    scores = masked_scores(query, key_all, key_mask)
    row_peak = jnp.max(scores, axis=-1, keepdims=True)
    log_total = row_peak + jnp.log(jnp.sum(jnp.exp(scores - row_peak), axis=-1, keepdims=True))
    probabilities = jnp.exp(scores - log_total).astype(jnp.bfloat16)
    attended_output = jnp.einsum(
        "shqk,skhd->sqhd", probabilities, split_heads(value_all), preferred_element_type=jnp.float32
    )
    return (attended_output.reshape(query.shape).astype(jnp.bfloat16), log_total)


def attention_backward(query, key_all, value_all, key_mask, log_total, grad_attended):
    scores = masked_scores(query, key_all, key_mask)
    probabilities = jnp.exp(scores - log_total)
    low_probs = probabilities.astype(jnp.bfloat16)
    grad_heads = split_heads(grad_attended)
    grad_probs = jnp.einsum(
        "sqhd,skhd->shqk", grad_heads, split_heads(value_all), preferred_element_type=jnp.float32
    )
    delta = jnp.sum(probabilities * grad_probs, axis=-1, keepdims=True)
    grad_scores = (probabilities * (grad_probs - delta)).astype(jnp.bfloat16)
    grad_query = jnp.einsum(
        "shqk,skhd->sqhd", grad_scores, split_heads(key_all), preferred_element_type=jnp.float32
    )
    grad_keys = jnp.einsum(
        "shqk,sqhd->skhd", grad_scores, split_heads(query), preferred_element_type=jnp.float32
    )
    grad_values = jnp.einsum(
        "shqk,sqhd->skhd", low_probs, grad_heads, preferred_element_type=jnp.float32
    )
    return (
        grad_query.reshape(query.shape),
        grad_keys.reshape(key_all.shape),
        grad_values.reshape(key_all.shape),
    )


def local(tokens, upstream, lengths, w_qkv, w_out, w_in, w_back, gain_attn, gain_ffn):
    section_count = lax.axis_size("section")
    section_index = lax.axis_index("section")
    micro_count, sequences, span_rows, model_width = tokens.shape
    head_count = model_width // HD
    key_count = span_rows * lax.axis_size("ctx")
    ctx_index = lax.axis_index("ctx")
    q_scale = HD ** (-0.5)
    qkv_low = w_qkv[0].astype(jnp.bfloat16)
    out_low = w_out[0].astype(jnp.bfloat16)
    in_low = w_in[0].astype(jnp.bfloat16)
    back_low = w_back[0].astype(jnp.bfloat16)
    attn_low = gain_attn[0].astype(jnp.bfloat16)
    ffn_low = gain_ffn[0].astype(jnp.bfloat16)
    (
        query_key_value_matrix,
        output_weight_matrix,
        input_weight_matrix,
        back_weight_matrix,
        gain_one,
        gain_two,
    ) = (
        lax.all_gather(qkv_low, ("dp", "ctx"), axis=0, tiled=True),
        lax.all_gather(out_low, ("dp", "ctx"), axis=0, tiled=True),
        lax.all_gather(in_low, ("dp", "ctx"), axis=0, tiled=True),
        lax.all_gather(back_low, ("dp", "ctx"), axis=0, tiled=True),
        lax.all_gather(attn_low, ("dp", "ctx"), axis=0, tiled=True),
        lax.all_gather(ffn_low, ("dp", "ctx"), axis=0, tiled=True),
    )
    gain_one = gain_one.astype(jnp.float32)
    gain_two = gain_two.astype(jnp.float32)
    positions = (ctx_index * span_rows + jnp.arange(span_rows)).astype(jnp.float32)
    cosine_tab, sine_tab = tables(positions)
    key_places = jnp.arange(key_count)
    row_total = sequences * span_rows
    span_shape = (sequences, span_rows, model_width)

    def scaled_rotate(tensor):
        return rotate(tensor, cosine_tab, sine_tab) * q_scale

    def plain_rotate(tensor):
        return rotate(tensor, cosine_tab, sine_tab)

    def mask_for(which_batch):
        lengths_now = lax.dynamic_index_in_dim(lengths, which_batch, 0, keepdims=False)
        return key_places[None, :] < lengths_now[:, None]

    moments = micro_count + section_count - 1
    acts = jnp.zeros((micro_count,) + span_shape, jnp.float32)
    inbound = jnp.zeros(span_shape, jnp.float32)
    stored = None
    for moment in range(moments):
        micro_index = moment - section_index
        in_range = (micro_index >= 0) & (micro_index < micro_count)
        which_batch = jnp.clip(micro_index, 0, micro_count - 1)
        fresh = lax.dynamic_index_in_dim(tokens, which_batch, 0, keepdims=False).astype(jnp.float32)
        source = jnp.where(section_index == 0, fresh, inbound)
        forward_residual_in = source.reshape(row_total, model_width)
        forward_normed_input = layer_norm(forward_residual_in, gain_one).astype(jnp.bfloat16)
        query_key_value_rows = jnp.dot(
            forward_normed_input, query_key_value_matrix, preferred_element_type=jnp.float32
        )
        query_key_value_rows = query_key_value_rows.reshape(sequences, span_rows, 3, head_count, HD)
        forward_query = (
            scaled_rotate(query_key_value_rows[:, :, 0]).astype(jnp.bfloat16).reshape(span_shape)
        )
        forward_key_rows = (
            plain_rotate(query_key_value_rows[:, :, 1]).astype(jnp.bfloat16).reshape(span_shape)
        )
        forward_value_rows = query_key_value_rows[:, :, 2].astype(jnp.bfloat16).reshape(span_shape)
        forward_key_all = lax.all_gather(forward_key_rows, "ctx", axis=1, tiled=True)
        forward_value_all = lax.all_gather(forward_value_rows, "ctx", axis=1, tiled=True)
        forward_attended_output, forward_log_total = attention_forward(
            forward_query, forward_key_all, forward_value_all, mask_for(which_batch)
        )
        forward_middle_state = forward_residual_in + jnp.dot(
            forward_attended_output.reshape(row_total, model_width),
            output_weight_matrix,
            preferred_element_type=jnp.float32,
        )
        forward_normed_second = layer_norm(forward_middle_state, gain_two).astype(jnp.bfloat16)
        forward_hidden_before_gelu = jnp.dot(
            forward_normed_second, input_weight_matrix, preferred_element_type=jnp.float32
        )
        forward_hidden_activation = jax.nn.gelu(
            forward_hidden_before_gelu, approximate=False
        ).astype(jnp.bfloat16)
        result = forward_middle_state + jnp.dot(
            forward_hidden_activation, back_weight_matrix, preferred_element_type=jnp.float32
        )
        forward_saved = (
            forward_residual_in,
            forward_query,
            forward_key_rows,
            forward_value_rows,
            forward_log_total,
            forward_attended_output,
            forward_middle_state,
            forward_hidden_before_gelu,
            forward_hidden_activation,
        )
        result, saved = (result.reshape(span_shape), forward_saved)
        if stored is None:
            stored = tuple((jnp.zeros((micro_count,) + item.shape, item.dtype) for item in saved))
        stored = tuple(
            (store(buffer, item, which_batch, in_range) for buffer, item in zip(stored, saved))
        )
        acts = store(acts, result, which_batch, in_range)
        if moment + 1 < moments:
            inbound = passed_along(result.astype(jnp.bfloat16), "section", 1).astype(result.dtype)
    grads_in = jnp.zeros((micro_count,) + span_shape, jnp.float32)
    inbound_grad = jnp.zeros(span_shape, jnp.float32)
    full_totals = (
        jnp.zeros(query_key_value_matrix.shape, jnp.float32),
        jnp.zeros(output_weight_matrix.shape, jnp.float32),
        jnp.zeros(input_weight_matrix.shape, jnp.float32),
        jnp.zeros(back_weight_matrix.shape, jnp.float32),
        jnp.zeros(gain_one.shape, jnp.float32),
        jnp.zeros(gain_two.shape, jnp.float32),
    )
    shard_totals = (
        jnp.zeros_like(w_qkv[0]),
        jnp.zeros_like(w_out[0]),
        jnp.zeros_like(w_in[0]),
        jnp.zeros_like(w_back[0]),
        jnp.zeros_like(gain_attn[0]),
        jnp.zeros_like(gain_ffn[0]),
    )
    for moment in range(moments):
        micro_index = moment - (section_count - 1 - section_index)
        in_range = (micro_index >= 0) & (micro_index < micro_count)
        which_batch = jnp.clip(micro_index, 0, micro_count - 1)
        fresh = lax.dynamic_index_in_dim(upstream, which_batch, 0, keepdims=False).astype(
            jnp.float32
        )
        incoming = jnp.where(section_index == section_count - 1, fresh, inbound_grad)
        saved = tuple(
            (lax.dynamic_index_in_dim(buffer, which_batch, 0, keepdims=False) for buffer in stored)
        )
        (
            residual_in,
            query,
            key_rows,
            value_rows,
            log_total,
            attended_output,
            middle_state,
            hidden_before_gelu,
            hidden_activation,
        ) = saved[:9]
        grad_top = incoming.reshape(row_total, model_width)
        low_top = grad_top.astype(jnp.bfloat16)
        grad_w_back = contract_rows(hidden_activation, low_top)
        grad_hidden = contract_cols(low_top, back_weight_matrix)
        gelu_primal, gelu_back = jax.vjp(
            partial(jax.nn.gelu, approximate=False), hidden_before_gelu
        )
        grad_pre = gelu_back(grad_hidden)[0].astype(jnp.bfloat16)
        normed_second, norm_two_back = jax.vjp(layer_norm, middle_state, gain_two)
        grad_w_in = contract_rows(normed_second.astype(jnp.bfloat16), grad_pre)
        grad_normed_two = contract_cols(grad_pre, input_weight_matrix)
        grad_mid_norm, grad_gain_two = norm_two_back(grad_normed_two)
        grad_middle = grad_top + grad_mid_norm
        low_middle = grad_middle.astype(jnp.bfloat16)
        grad_w_out = contract_rows(attended_output.reshape(row_total, model_width), low_middle)
        grad_attended = (
            contract_cols(low_middle, output_weight_matrix).astype(jnp.bfloat16).reshape(span_shape)
        )
        key_all = lax.all_gather(key_rows, "ctx", axis=1, tiled=True)
        value_all = lax.all_gather(value_rows, "ctx", axis=1, tiled=True)
        grad_query, grad_keys, grad_values = attention_backward(
            query, key_all, value_all, mask_for(which_batch), log_total, grad_attended
        )
        grad_keys, grad_values = (
            lax.psum_scatter(
                grad_keys.astype(jnp.bfloat16), "ctx", scatter_dimension=1, tiled=True
            ).astype(jnp.float32),
            lax.psum_scatter(
                grad_values.astype(jnp.bfloat16), "ctx", scatter_dimension=1, tiled=True
            ).astype(jnp.float32),
        )
        heads_shape = (sequences, span_rows, head_count, HD)
        zero_heads = jnp.zeros(heads_shape, jnp.float32)
        rotated_q, q_back = jax.vjp(scaled_rotate, zero_heads)
        rotated_k, k_back = jax.vjp(plain_rotate, zero_heads)
        low_query = grad_query.astype(jnp.bfloat16).astype(jnp.float32).reshape(heads_shape)
        low_keys = grad_keys.astype(jnp.bfloat16).astype(jnp.float32).reshape(heads_shape)
        part_q = q_back(low_query)[0]
        part_k = k_back(low_keys)[0]
        part_v = grad_values.reshape(heads_shape)
        grad_qkv = (
            jnp.stack([part_q, part_k, part_v], axis=2)
            .reshape(row_total, 3 * model_width)
            .astype(jnp.bfloat16)
        )
        normed_input, norm_one_back = jax.vjp(layer_norm, residual_in, gain_one)
        grad_w_qkv = contract_rows(normed_input.astype(jnp.bfloat16), grad_qkv)
        grad_normed = contract_cols(grad_qkv, query_key_value_matrix)
        grad_in_norm, grad_gain_one = norm_one_back(grad_normed)
        grad_source = grad_middle + grad_in_norm
        partial_grads = (
            grad_w_qkv,
            grad_w_out,
            grad_w_in,
            grad_w_back,
            grad_gain_one,
            grad_gain_two,
        )
        grad_source, partial_grads = (grad_source.reshape(span_shape), partial_grads)
        g_qkv, g_out, g_in, g_back, g_one, g_two = tuple(
            (jnp.where(in_range, item, 0.0) for item in partial_grads)
        )
        grads_in = store(grads_in, grad_source, which_batch, in_range)
        full_totals = tuple(
            (
                total + item
                for total, item in zip(full_totals, (g_qkv, g_out, g_in, g_back, g_one, g_two))
            )
        )
        if moment + 1 < moments:
            inbound_grad = passed_along(grad_source.astype(jnp.bfloat16), "section", -1).astype(
                grad_source.dtype
            )
    sum_qkv, sum_out, sum_in, sum_back, sum_one, sum_two = full_totals
    shard_totals = (
        lax.psum_scatter(sum_qkv, ("dp", "ctx"), scatter_dimension=0, tiled=True),
        lax.psum_scatter(sum_out, ("dp", "ctx"), scatter_dimension=0, tiled=True),
        lax.psum_scatter(sum_in, ("dp", "ctx"), scatter_dimension=0, tiled=True),
        lax.psum_scatter(sum_back, ("dp", "ctx"), scatter_dimension=0, tiled=True),
        lax.psum_scatter(sum_one, ("dp", "ctx"), scatter_dimension=0, tiled=True),
        lax.psum_scatter(sum_two, ("dp", "ctx"), scatter_dimension=0, tiled=True),
    )
    return (
        acts[None],
        grads_in[None],
        shard_totals[0][None],
        shard_totals[1][None],
        shard_totals[2][None],
        shard_totals[3][None],
        shard_totals[4][None],
        shard_totals[5][None],
    )


def solution(mesh):
    return jax.shard_map(
        local,
        mesh=mesh,
        in_specs=(
            P(None, "dp", "ctx", None),
            P(None, "dp", "ctx", None),
            P(None, "dp"),
            P("section", ("dp", "ctx"), None),
            P("section", ("dp", "ctx"), None),
            P("section", ("dp", "ctx"), None),
            P("section", ("dp", "ctx"), None),
            P("section", ("dp", "ctx")),
            P("section", ("dp", "ctx")),
        ),
        out_specs=(
            P("section", None, "dp", "ctx", None),
            P("section", None, "dp", "ctx", None),
            P("section", ("dp", "ctx"), None),
            P("section", ("dp", "ctx"), None),
            P("section", ("dp", "ctx"), None),
            P("section", ("dp", "ctx"), None),
            P("section", ("dp", "ctx")),
            P("section", ("dp", "ctx")),
        ),
        check_vma=False,
    )
```

profile of v0, /device:TPU:0, one launch (start us, length us, event | category | flops | bytes accessed | tf_op | source)
XLA Modules:
  0.0 2275.4 jit_solution(7702583870397529192)
XLA Ops:
  12.7 44.1 %all-reduce.17 = (bf16[768]{0:T(1024)(128)(2,1)S(1)}, bf16[768]{0:T(1024)(128)(2,1)S(1)}) all-reduce(bf16[768]{0:T(1024)(128)(2,1)S(1)} %dynamic-update-slice, bf16[768]{0:T(1024)(128)(2,1)S(1)} %dynamic-update-slice.1), channel_id=2, replica_groups=mesh['section'=2,'dp'=4,'ctx'=4] {'dp','ctx'}, use_global_device_ids=true, to_apply=%add.12 | all-reduce | flops 1536 | bytes 6144
  62.2 23.0 %all-gather.41.cloned.1.call-done = bf16[1,768,2304]{2,1,0:T(8,128)(2,1)} async-done(((bf16[1,48,2304]{2,1,0:T(8,128)(2,1)}), bf16[1,768,2304]{2,1,0:T(8,128)(2,1)}) %all-gather.41.cloned.1.call-update) | async-done | bytes 3538960 | tf_op jit(solution)/shard_map/all_gather | solution.py:128
  85.3 5.9 copy.104
  109.0 54.5 %all-gather.31.cloned.1.call-done = bf16[2,1024,768]{1,2,0:T(8,128)(2,1)} async-done(((bf16[2,256,768]{1,2,0:T(8,128)(2,1)}), bf16[2,1024,768]{1,2,0:T(8,128)(2,1)}) %all-gather.31.cloned.1.call-update) | async-done | bytes 3145744 | tf_op jit(solution)/shard_map/all_gather | solution.py:176
  163.5 14.9 select_reduce_fusion.2
  178.4 11.1 exponential_reduce_fusion.2
  189.6 37.1 %all-gather.29.cloned.1.call-done = bf16[2,1024,768]{1,2,0:T(8,128)(2,1)} async-done(((bf16[2,256,768]{1,2,0:T(8,128)(2,1)}), bf16[2,1024,768]{1,2,0:T(8,128)(2,1)}) %all-gather.29.cloned.1.call-update) | async-done | bytes 3145744 | tf_op jit(solution)/shard_map/all_gather | solution.py:177
  226.7 12.5 broadcast_select_fusion.2
  241.1 43.2 %all-gather.43.cloned.1.call-done = bf16[1,768,768]{2,1,0:T(8,128)(2,1)} async-done(((bf16[1,48,768]{2,1,0:T(8,128)(2,1)}), bf16[1,768,768]{2,1,0:T(8,128)(2,1)}) %all-gather.43.cloned.1.call-update) | async-done | bytes 1179664 | tf_op jit(solution)/shard_map/all_gather | solution.py:129
  287.5 79.3 %all-gather.45.cloned.1.call-done = bf16[1,768,3072]{2,1,0:T(8,128)(2,1)} async-done(((bf16[1,48,3072]{2,1,0:T(8,128)(2,1)}), bf16[1,768,3072]{2,1,0:T(8,128)(2,1)}) %all-gather.45.cloned.1.call-update) | async-done | bytes 4718608 | tf_op jit(solution)/shard_map/all_gather | solution.py:130
  370.7 21.0 bitcast_dynamic-update-slice_fusion.5
  391.7 57.5 %all-gather.47.cloned.1.call-done = bf16[1,3072,768]{2,1,0:T(8,128)(2,1)} async-done(((bf16[1,192,768]{2,1,0:T(8,128)(2,1)}), bf16[1,3072,768]{2,1,0:T(8,128)(2,1)}) %all-gather.47.cloned.1.call-update) | async-done | bytes 4718608 | tf_op jit(solution)/shard_map/all_gather | solution.py:131
  449.1 7.2 fusion.397
  476.4 54.9 %all-gather.35.cloned.1.call-done = bf16[2,1024,768]{1,2,0:T(8,128)(2,1)} async-done(((bf16[2,256,768]{1,2,0:T(8,128)(2,1)}), bf16[2,1024,768]{1,2,0:T(8,128)(2,1)}) %all-gather.35.cloned.1.call-update) | async-done | bytes 3145744 | tf_op jit(solution)/shard_map/all_gather | solution.py:176
  531.3 15.3 select_reduce_fusion.1
  546.5 11.3 exponential_reduce_fusion.1
  557.9 36.5 %all-gather.33.cloned.1.call-done = bf16[2,1024,768]{1,2,0:T(8,128)(2,1)} async-done(((bf16[2,256,768]{1,2,0:T(8,128)(2,1)}), bf16[2,1024,768]{1,2,0:T(8,128)(2,1)}) %all-gather.33.cloned.1.call-update) | async-done | bytes 3145744 | tf_op jit(solution)/shard_map/all_gather | solution.py:177
  594.5 11.6 fusion.215
  609.6 20.3 bitcast_dynamic-update-slice_fusion.4
  736.7 6.2 bitcast_dynamic-update-slice_fusion.1
  754.5 14.9 select_reduce_fusion
  769.3 11.6 exponential_reduce_fusion
  781.0 11.8 fusion.214
  802.0 20.0 bitcast_dynamic-update-slice_fusion.3
  826.7 18.8 fusion.43
  857.5 12.2 fusion.403
  869.7 29.4 %all-gather.51.cloned.1.call-done = bf16[1,2,1024,768]{3,2,1,0:T(8,128)(2,1)} async-done(((bf16[1,2,256,768]{3,2,1,0:T(8,128)(2,1)}), bf16[1,2,1024,768]{3,2,1,0:T(8,128)(2,1)}) %all-gather.51.cloned.1.call-update) | async-done | bytes 3145744 | tf_op jit(solution)/shard_map/all_gather | solution.py:275
  902.4 17.2 multiply_reduce_fusion.2
  919.6 16.9 multiply_convert_fusion.2
  943.1 12.3 fusion.170
  959.5 9.5 bitcast_multiply_fusion.13
  975.7 50.8 %all-gather.55.cloned.1.call-done = bf16[1,2,1024,768]{3,2,1,0:T(8,128)(2,1)} async-done(((bf16[1,2,256,768]{3,2,1,0:T(8,128)(2,1)}), bf16[1,2,1024,768]{3,2,1,0:T(8,128)(2,1)}) %all-gather.55.cloned.1.call-update) | async-done | bytes 3145744 | tf_op jit(solution)/shard_map/all_gather | solution.py:275
  1031.2 56.5 %reduce-scatter.11.cloned.1.call-done = bf16[2,256,768]{1,2,0:T(8,128)(2,1)} async-done(((bf16[2,1024,768]{1,2,0:T(8,128)(2,1)}), bf16[2,256,768]{1,2,0:T(8,128)(2,1)}) %reduce-scatter.11.cloned.1.call-update) | async-done | bytes 786448 | tf_op jit(solution)/shard_map/reduce_scatter | solution.py:280
  1090.5 59.7 %reduce-scatter.13.cloned.1.call-done = bf16[2,256,768]{1,2,0:T(8,128)(2,1)} async-done(((bf16[2,1024,768]{1,2,0:T(8,128)(2,1)}), bf16[2,256,768]{1,2,0:T(8,128)(2,1)}) %reduce-scatter.13.cloned.1.call-update) | async-done | bytes 786448 | tf_op jit(solution)/shard_map/reduce_scatter | solution.py:283
  1165.2 11.1 fusion.404
  1177.6 17.8 fusion.48
  1202.3 17.9 multiply_reduce_fusion.1
  1220.1 17.5 multiply_convert_fusion.1
  1243.1 12.3 fusion.173
  1261.4 17.3 all-gather.59.cloned.1.call-done
  1283.4 10.1 bitcast_multiply_fusion.11
  1295.5 44.4 %reduce-scatter.15.cloned.1.call-done = bf16[2,256,768]{1,2,0:T(8,128)(2,1)} async-done(((bf16[2,1024,768]{1,2,0:T(8,128)(2,1)}), bf16[2,256,768]{1,2,0:T(8,128)(2,1)}) %reduce-scatter.15.cloned.1.call-update) | async-done | bytes 786448 | tf_op jit(solution)/shard_map/reduce_scatter | solution.py:280
  1342.8 59.6 %reduce-scatter.17.cloned.1.call-done = bf16[2,256,768]{1,2,0:T(8,128)(2,1)} async-done(((bf16[2,1024,768]{1,2,0:T(8,128)(2,1)}), bf16[2,256,768]{1,2,0:T(8,128)(2,1)}) %reduce-scatter.17.cloned.1.call-update) | async-done | bytes 786448 | tf_op jit(solution)/shard_map/reduce_scatter | solution.py:283
  1416.7 11.0 fusion.405
  1429.0 18.0 fusion.53
  1459.6 18.2 multiply_reduce_fusion
  1477.8 16.7 multiply_convert_fusion
  1500.1 13.0 fusion.176
  1535.3 4.9 fusion.263
  1540.2 5.4 fusion.264
  1545.6 8.9 select_add_fusion.1
  1555.6 4.7 fusion.165
  1560.4 4.8 fusion.163
  1565.2 9.1 select_add_fusion
  1576.2 7.1 fusion.256
  1583.3 5.2 fusion.259
  1588.5 8.6 bitcast_multiply_fusion.9
  1601.9 22.6 reduce-scatter.21.cloned.1.call-done
  1630.9 8.6 select_add_fusion.2
  1659.9 42.1 %all-reduce.16 = (f32[768]{0:T(1024)S(1)}, f32[768]{0:T(1024)S(1)}) all-reduce(f32[768]{0:T(1024)S(1)} %select_add_fusion.5, f32[768]{0:T(1024)S(1)} %select_add_fusion.4), channel_id=24, replica_groups=mesh['section'=2,'dp'=4,'ctx'=4] {'dp','ctx'}, use_global_device_ids=true, to_apply=%region_58.59.clone | all-reduce | flops 1536 | bytes 12288
  1708.4 49.4 %reduce-scatter.25.cloned.1.call-done = f32[48,768]{1,0:T(8,128)} async-done(((f32[768,768]{1,0:T(8,128)}), f32[48,768]{1,0:T(8,128)}) %reduce-scatter.25.cloned.1.call-update) | async-done | bytes 147472 | tf_op jit(solution)/shard_map/reduce_scatter | solution.py:332
  1757.8 177.4 %reduce-scatter.27.cloned.1.call-done = f32[48,3072]{1,0:T(8,128)} async-done(((f32[768,3072]{1,0:T(8,128)}), f32[48,3072]{1,0:T(8,128)}) %reduce-scatter.27.cloned.1.call-update) | async-done | bytes 589840 | tf_op jit(solution)/shard_map/reduce_scatter | solution.py:333
  1935.2 176.4 %reduce-scatter.29.cloned.1.call-done = f32[192,768]{1,0:T(8,128)} async-done(((f32[3072,768]{1,0:T(8,128)}), f32[192,768]{1,0:T(8,128)}) %reduce-scatter.29.cloned.1.call-update) | async-done | bytes 589840 | tf_op jit(solution)/shard_map/reduce_scatter | solution.py:334
  2111.6 156.8 %reduce-scatter.23.cloned.1.call-done = f32[48,2304]{1,0:T(8,128)} async-done(((f32[768,2304]{1,0:T(8,128)}), f32[48,2304]{1,0:T(8,128)}) %reduce-scatter.23.cloned.1.call-update) | async-done | bytes 442384 | tf_op jit(solution)/shard_map/reduce_scatter | solution.py:331
  (757 shorter events, 370.7 us)
Async XLA Ops:
  7.2 78.1 %all-gather.41.cloned.1.call-start = ((), (), s32[]{:S(2)}) async-start(), calls=%async_computation.26 | async-start | bytes 3760128 | tf_op jit(solution)/shard_map/all_gather | solution.py:128
  9.0 154.6 %all-gather.31.cloned.1.call-start = ((), (), s32[]{:S(2)}) async-start(), calls=%async_computation.11 | async-start | bytes 3932160 | tf_op jit(solution)/shard_map/all_gather | solution.py:176
  56.8 581.6 %copy-start.139 = (f32[768]{0:T(1024)}, f32[768]{0:T(1024)S(1)}, u32[]{:S(2)}) copy-start(f32[768]{0:T(1024)S(1)} %convert_element_type.771) | copy-start | bytes 9220
  59.1 472.2 %copy-start.64 = (f32[256,64]{0,1:T(8,128)}, f32[256,64]{0,1:T(8,128)S(1)}, u32[]{:S(2)}) copy-start(f32[256,64]{0,1:T(8,128)S(1)} %get-tuple-element.135) | copy-start | bytes 196612
  59.1 472.2 %copy-start.69 = (f32[256,64]{0,1:T(8,128)}, f32[256,64]{0,1:T(8,128)S(1)}, u32[]{:S(2)}) copy-start(f32[256,64]{0,1:T(8,128)S(1)} %get-tuple-element.134) | copy-start | bytes 196612
  101.4 125.3 %all-gather.29.cloned.1.call-start = ((), (), s32[]{:S(2)}) async-start(), calls=%async_computation.10 | async-start | bytes 3932160 | tf_op jit(solution)/shard_map/all_gather | solution.py:177
  104.2 180.1 %all-gather.43.cloned.1.call-start = ((), (), s32[]{:S(2)}) async-start(), calls=%async_computation.27 | async-start | bytes 1253376 | tf_op jit(solution)/shard_map/all_gather | solution.py:129
  105.0 261.9 %all-gather.45.cloned.1.call-start = ((), (), s32[]{:S(2)}) async-start(), calls=%async_computation.28 | async-start | bytes 5013504 | tf_op jit(solution)/shard_map/all_gather | solution.py:130
  105.8 343.3 %all-gather.47.cloned.1.call-start = ((), (), s32[]{:S(2)}) async-start(), calls=%async_computation.29 | async-start | bytes 5013504 | tf_op jit(solution)/shard_map/all_gather | solution.py:131
  106.6 424.7 %all-gather.35.cloned.1.call-start = ((), (), s32[]{:S(2)}) async-start(), calls=%async_computation.13 | async-start | bytes 3932160 | tf_op jit(solution)/shard_map/all_gather | solution.py:176
  107.4 741.9 %copy-start.126 = (f32[768]{0:T(1024)}, f32[768]{0:T(1024)S(1)}, u32[]{:S(2)}) copy-start(f32[768]{0:T(1024)S(1)} %convert_element_type.772) | copy-start | bytes 9220
  109.0 69.4 %copy-start.76 = (f32[2,256,12,32]{1,3,2,0:T(8,128)}, f32[2,256,12,32]{1,3,2,0:T(8,128)S(1)}, u32[]{:S(2)}) copy-start(f32[2,256,12,32]{1,3,2,0:T(8,128)S(1)} %get-tuple-element.125) | copy-start | bytes 2359300
  109.0 69.4 %copy-start.77 = (f32[2,256,12,32]{1,3,2,0:T(8,128)}, f32[2,256,12,32]{1,3,2,0:T(8,128)S(1)}, u32[]{:S(2)}) copy-start(f32[2,256,12,32]{1,3,2,0:T(8,128)S(1)} %get-tuple-element.126) | copy-start | bytes 2359300
  287.2 161.9 %copy-start.35 = (f32[512,768]{1,0:T(8,128)}, f32[512,768]{1,0:T(8,128)S(1)}, u32[]{:S(2)}) copy-start(f32[512,768]{1,0:T(8,128)S(1)} %get-tuple-element.147) | copy-start | bytes 4718596
  456.3 3.4 collective-permute-start
  460.0 147.1 %copy-start.22 = (f32[2,256,768]{2,1,0:T(8,128)}, f32[2,256,768]{2,1,0:T(8,128)S(1)}, u32[]{:S(2)}) copy-start(f32[2,256,768]{2,1,0:T(8,128)S(1)} %get-tuple-element.69) | copy-start | bytes 4718596
  468.5 125.9 %all-gather.33.cloned.1.call-start = ((), (), s32[]{:S(2)}) async-start(), calls=%async_computation.12 | async-start | bytes 3932160 | tf_op jit(solution)/shard_map/all_gather | solution.py:177
  471.0 283.4 %all-gather.39.cloned.1.call-start = ((), (), s32[]{:S(2)}) async-start(), calls=%async_computation.15 | async-start | bytes 3932160 | tf_op jit(solution)/shard_map/all_gather | solution.py:176
  557.9 48.2 %copy-start.132 = (f32[2,2,12,256,1]{3,2,1,4,0:T(8,128)}, f32[2,2,12,256,1]{3,2,1,4,0:T(8,128)S(1)}, u32[]{:S(2)}) copy-start(f32[2,2,12,256,1]{3,2,1,4,0:T(8,128)S(1)} %get-tuple-element.60) | copy-start | bytes 147460
  607.7 22.2 slice-start.11
  608.6 21.2 copy-start.40
  609.6 20.3 slice-start.12
  633.7 4.1 collective-permute-start.1
  647.4 133.6 %all-gather.37.cloned.1.call-start = ((), (), s32[]{:S(2)}) async-start(), calls=%async_computation.14 | async-start | bytes 3932160 | tf_op jit(solution)/shard_map/all_gather | solution.py:177
  649.9 204.4 %all-gather.49.cloned.1.call-start = ((), (), s32[]{:S(2)}) async-start(), calls=%async_computation.30 | async-start | bytes 3932160 | tf_op jit(solution)/shard_map/all_gather | solution.py:274
  706.8 192.4 %all-gather.51.cloned.1.call-start = ((), (), s32[]{:S(2)}) async-start(), calls=%async_computation.31 | async-start | bytes 3932160 | tf_op jit(solution)/shard_map/all_gather | solution.py:275
  714.0 257.1 %all-gather.53.cloned.1.call-start = ((), (), s32[]{:S(2)}) async-start(), calls=%async_computation.32 | async-start | bytes 3932160 | tf_op jit(solution)/shard_map/all_gather | solution.py:274
  719.9 306.6 %all-gather.55.cloned.1.call-start = ((), (), s32[]{:S(2)}) async-start(), calls=%async_computation.33 | async-start | bytes 3932160 | tf_op jit(solution)/shard_map/all_gather | solution.py:275
  754.4 333.3 %reduce-scatter.11.cloned.1.call-start = ((), (), s32[]{:S(2)}) async-start(), calls=%async_computation.16 | async-start | bytes 3932160 | tf_op jit(solution)/shard_map/reduce_scatter | solution.py:280
  798.4 23.7 %slice-start = ((s8[12582912]{0:T(1024)(128)(4,1)}), s8[4194304]{0:T(1024)(128)(4,1)S(1)}, s32[]{:S(2)}) async-start(s8[12582912]{0:T(1024)(128)(4,1)} %bitcast.845), calls=%async_computation.36 | async-start | bytes 8388608
  800.0 22.0 copy-start.149
  800.3 21.7 copy-start.172
  802.0 20.1 slice-start.1
  802.0 20.1 slice-start.2
  822.1 23.4 %slice-start.15 = ((s8[4718592]{0:T(1024)(128)(4,1)}), s8[4194304]{0:T(1024)(128)(4,1)S(1)}, s32[]{:S(2)}) async-start(s8[4718592]{0:T(1024)(128)(4,1)} %bitcast.960), calls=%async_computation.51 | async-start | bytes 8388608
  869.7 32.6 %copy-start.148 = (pred[2,1024]{1,0:T(4,128)(4,1)S(1)}, pred[2,1024]{1,0:T(4,128)(4,1)}, u32[]{:S(2)}) copy-start(pred[2,1024]{1,0:T(4,128)(4,1)} %iota_compare_fusion.2) | copy-start | bytes 6148
  942.0 208.1 %reduce-scatter.13.cloned.1.call-start = ((), (), s32[]{:S(2)}) async-start(), calls=%async_computation.17 | async-start | bytes 3932160 | tf_op jit(solution)/shard_map/reduce_scatter | solution.py:283
  955.4 302.4 %all-gather.57.cloned.1.call-start = ((), (), s32[]{:S(2)}) async-start(), calls=%async_computation.34 | async-start | bytes 3932160 | tf_op jit(solution)/shard_map/all_gather | solution.py:274
  956.0 322.7 %all-gather.59.cloned.1.call-start = ((), (), s32[]{:S(2)}) async-start(), calls=%async_computation.35 | async-start | bytes 3932160 | tf_op jit(solution)/shard_map/all_gather | solution.py:275
  958.6 381.3 %reduce-scatter.15.cloned.1.call-start = ((), (), s32[]{:S(2)}) async-start(), calls=%async_computation.18 | async-start | bytes 3932160 | tf_op jit(solution)/shard_map/reduce_scatter | solution.py:280
  959.1 201.6 %copy-start.159 = (f32[512]{0:T(512)}, f32[512]{0:T(512)S(1)}, u32[]{:S(2)}) copy-start(f32[512]{0:T(512)S(1)} %broadcast_multiply_fusion.7) | copy-start | bytes 6148
  959.4 201.3 %copy-start.161 = (f32[512]{0:T(512)}, f32[512]{0:T(512)S(1)}, u32[]{:S(2)}) copy-start(f32[512]{0:T(512)S(1)} %fusion.347) | copy-start | bytes 6148
  959.5 195.5 %copy-start.168 = (f32[512]{0:T(512)}, f32[512]{0:T(512)S(1)}, u32[]{:S(2)}) copy-start(f32[512]{0:T(512)S(1)} %broadcast_multiply_fusion.3) | copy-start | bytes 6148
  959.5 195.5 %copy-start.163 = (f32[512]{0:T(512)}, f32[512]{0:T(512)S(1)}, u32[]{:S(2)}) copy-start(f32[512]{0:T(512)S(1)} %broadcast_multiply_fusion.5) | copy-start | bytes 6148
  969.2 229.7 %copy-start.157 = (f32[512]{0:T(512)}, f32[512]{0:T(512)S(1)}, u32[]{:S(2)}) copy-start(f32[512]{0:T(512)S(1)} %fusion.348) | copy-start | bytes 6148
  975.7 111.9 %copy-start.71 = (f32[256,64]{0,1:T(8,128)S(1)}, f32[256,64]{0,1:T(8,128)}, u32[]{:S(2)}) copy-start(f32[256,64]{0,1:T(8,128)} %copy-done.69) | copy-start | bytes 196612
  1031.2 58.0 %copy-start.66 = (f32[256,64]{0,1:T(8,128)S(1)}, f32[256,64]{0,1:T(8,128)}, u32[]{:S(2)}) copy-start(f32[256,64]{0,1:T(8,128)} %copy-done.64) | copy-start | bytes 196612
  1163.6 12.7 collective-permute-start.2
  1243.1 159.3 %reduce-scatter.17.cloned.1.call-start = ((), (), s32[]{:S(2)}) async-start(), calls=%async_computation.19 | async-start | bytes 3932160 | tf_op jit(solution)/shard_map/reduce_scatter | solution.py:283
  1255.5 343.6 %reduce-scatter.19.cloned.1.call-start = ((), (), s32[]{:S(2)}) async-start(), calls=%async_computation.20 | async-start | bytes 3932160 | tf_op jit(solution)/shard_map/reduce_scatter | solution.py:280
  1261.4 155.3 %copy-start.16 = (bf16[1,2,1024,768]{2,3,1,0:T(8,128)(2,1)}, bf16[1,2,1024,768]{2,3,1,0:T(8,128)(2,1)S(1)}, u32[]{:S(2)}) copy-start(bf16[1,2,1024,768]{2,3,1,0:T(8,128)(2,1)S(1)} %copy.141) | copy-start | bytes 9437188
  1261.4 22.0 copy-start.176
  1261.4 22.0 copy-start.177
  1261.4 22.0 copy-start.106
  1283.4 129.0 %copy-start.166 = (f32[512]{0:T(512)}, f32[512]{0:T(512)S(1)}, u32[]{:S(2)}) copy-start(f32[512]{0:T(512)S(1)} %fusion.349) | copy-start | bytes 6148
  1293.5 46.5 %copy-start.72 = (f32[256,64]{0,1:T(8,128)S(1)}, f32[256,64]{0,1:T(8,128)}, u32[]{:S(2)}) copy-start(f32[256,64]{0,1:T(8,128)} %copy-done.69) | copy-start | bytes 196612
  1295.5 46.0 %copy-start.67 = (f32[256,64]{0,1:T(8,128)S(1)}, f32[256,64]{0,1:T(8,128)}, u32[]{:S(2)}) copy-start(f32[256,64]{0,1:T(8,128)} %copy-done.64) | copy-start | bytes 196612
  1415.2 12.5 collective-permute-start.3
  1427.7 19.3 slice-start.19
  1500.1 124.5 %reduce-scatter.21.cloned.1.call-start = ((), (), s32[]{:S(2)}) async-start(), calls=%async_computation.21 | async-start | bytes 3932160 | tf_op jit(solution)/shard_map/reduce_scatter | solution.py:283
  1513.2 244.6 %reduce-scatter.25.cloned.1.call-start = ((), (), s32[]{:S(2)}) async-start(), calls=%async_computation.23 | async-start | bytes 2506752 | tf_op jit(solution)/shard_map/reduce_scatter | solution.py:332
  1535.2 400.0 %reduce-scatter.27.cloned.1.call-start = ((), (), s32[]{:S(2)}) async-start(), calls=%async_computation.24 | async-start | bytes 10027008 | tf_op jit(solution)/shard_map/reduce_scatter | solution.py:333
  1554.5 557.1 %reduce-scatter.29.cloned.1.call-start = ((), (), s32[]{:S(2)}) async-start(), calls=%async_computation.25 | async-start | bytes 10027008 | tf_op jit(solution)/shard_map/reduce_scatter | solution.py:334
  1574.3 694.1 %reduce-scatter.23.cloned.1.call-start = ((), (), s32[]{:S(2)}) async-start(), calls=%async_computation.22 | async-start | bytes 7520256 | tf_op jit(solution)/shard_map/reduce_scatter | solution.py:331
  (179 other events, 922.0 us)
Sparse Core Ops, SparseCore 0:
  11.3 73.9 all-gather.40
  101.5 61.9 all-gather.30
  165.1 61.5 all-gather.28
  229.9 54.3 all-gather.42
  287.5 79.3 all-gather.44
  370.0 79.0 all-gather.46
  468.7 62.5 all-gather.34
  532.8 61.6 all-gather.32
  647.5 61.6 all-gather.38
  710.6 61.6 all-gather.36
  773.9 61.6 all-gather.48
  837.0 62.1 all-gather.50
  900.7 62.1 all-gather.52
  964.3 62.1 all-gather.54
  1028.7 58.9 reduce-scatter.10
  1089.8 60.2 reduce-scatter.12
  1151.5 63.4 all-gather.56
  1216.5 62.1 all-gather.58
  1281.0 58.9 reduce-scatter.14
  1342.1 60.2 reduce-scatter.16
  1500.2 61.1 reduce-scatter.18
  1564.2 60.2 reduce-scatter.20
  1630.0 127.7 reduce-scatter.24
  1764.8 170.3 reduce-scatter.26
  1941.5 170.1 reduce-scatter.28
  2118.2 150.1 reduce-scatter.22
where the time goes:
time: 2290 us; the launch traced here: 2280 us
  waiting for transfers between devices  1290 us (56%)
  matrix products  477 us (21%)
  local copies, waits for them, and re-layouts  204 us (9%)
  other arithmetic  188 us (8%)
  blocking collectives  86.2 us (4%)
    reduce_scatter x1, waiting for transfers between devices, local(): lax.psum_scatter(sum_in, ('dp', 'ctx'), scatter_dimension=0, tiled=True)  177 us
    reduce_scatter x1, waiting for transfers between devices, local(): lax.psum_scatter(sum_back, ('dp', 'ctx'), scatter_dimension=0, tiled=True)  176 us
    reduce_scatter x1, waiting for transfers between devices, local(): lax.psum_scatter(sum_qkv, ('dp', 'ctx'), scatter_dimension=0, tiled=True)  157 us
    reduce_scatter x3, waiting for transfers between devices, local(): lax.psum_scatter(grad_values.astype(jnp.bfloat16), 'ctx', scatter_dimensi...  142 us
    all_gather x3, waiting for transfers between devices, local(): lax.all_gather(forward_key_rows, 'ctx', axis=1, tiled=True)  109 us
    reduce_scatter x3, waiting for transfers between devices, local(): lax.psum_scatter(grad_keys.astype(jnp.bfloat16), 'ctx', scatter_dimension...  101 us
    all_gather x3, waiting for transfers between devices, local(): value_all = lax.all_gather(value_rows, 'ctx', axis=1, tiled=True)  97.5 us
    unnamed x2, blocking collectives  86.2 us
  transfers between devices with their start and end apart: 30, of which 22 were waited for; matrix products, arithmetic and copies ran while one was open for 29% of the time, Pallas kernels for 0%

commit v1 on v0

--- a/solution.py
+++ b/solution.py
@@ -5,6 +5,11 @@
 from jax.sharding import PartitionSpec as P
 
 HD = 64
+advance_blocks = lambda payload, array_here: jnp.split(
+    lax.all_gather(jnp.concatenate([payload, array_here], axis=0), "ctx", axis=1, tiled=True),
+    [payload.shape[0]],
+    axis=0,
+)
 
 
 def passed_along(value, axis, steps):
@@ -173,8 +178,7 @@
             plain_rotate(query_key_value_rows[:, :, 1]).astype(jnp.bfloat16).reshape(span_shape)
         )
         forward_value_rows = query_key_value_rows[:, :, 2].astype(jnp.bfloat16).reshape(span_shape)
-        forward_key_all = lax.all_gather(forward_key_rows, "ctx", axis=1, tiled=True)
-        forward_value_all = lax.all_gather(forward_value_rows, "ctx", axis=1, tiled=True)
+        forward_key_all, forward_value_all = advance_blocks(forward_key_rows, forward_value_rows)
         forward_attended_output, forward_log_total = attention_forward(
             forward_query, forward_key_all, forward_value_all, mask_for(which_batch)
         )

time: 2290 us -> 2380 us (1.039)
  waiting for transfers between devices: 1290 us -> 1380 us
    all_gather x6 -> x3, waiting for transfers between devices: 183 us -> 309 us  [lax.all_gather(jnp.concatenate([payload, array_here], axis=0), 'ctx', axi...]
    reduce_scatter x3, waiting for transfers between devices: 101 us -> 54.4 us  [local(): lax.psum_scatter(grad_keys.astype(jnp.bfloat16), 'ctx', scatter_dimension...]
    all_gather x3, waiting for transfers between devices: 97.5 us -> 124 us  [local(): value_all = lax.all_gather(value_rows, 'ctx', axis=1, tiled=True)]
    all_gather x1, waiting for transfers between devices: 43.2 us -> 18 us  [local(): lax.all_gather(out_low, ('dp', 'ctx'), axis=0, tiled=True)]
    unnamed x439 -> x437, local copies, waits for them, and re-layouts: 59 us -> 58.5 us
  transfers between devices with their start and end apart: 30 -> 27, of which waited for: 22 -> 21; matrix products, arithmetic and copies ran while one was open for 29% -> 26% of each run, Pallas kernels for 0% -> 0%
where the time goes in v1:
time: 2380 us; the launch traced here: 2370 us
  waiting for transfers between devices  1380 us (58%)
  matrix products  471 us (20%)
  local copies, waits for them, and re-layouts  220 us (9%)
  other arithmetic  189 us (8%)
  blocking collectives  86.1 us (4%)
    all_gather x3, waiting for transfers between devices, lax.all_gather(jnp.concatenate([payload, array_here], axis=0), 'ctx', axi...  309 us
    reduce_scatter x1, waiting for transfers between devices, local(): lax.psum_scatter(sum_in, ('dp', 'ctx'), scatter_dimension=0, tiled=True)  177 us
    reduce_scatter x1, waiting for transfers between devices, local(): lax.psum_scatter(sum_back, ('dp', 'ctx'), scatter_dimension=0, tiled=True)  177 us
    reduce_scatter x1, waiting for transfers between devices, local(): lax.psum_scatter(sum_qkv, ('dp', 'ctx'), scatter_dimension=0, tiled=True)  157 us
    reduce_scatter x3, waiting for transfers between devices, local(): lax.psum_scatter(grad_values.astype(jnp.bfloat16), 'ctx', scatter_dimensi...  140 us
    all_gather x3, waiting for transfers between devices, local(): value_all = lax.all_gather(value_rows, 'ctx', axis=1, tiled=True)  124 us
    unnamed x2, blocking collectives  86.1 us
    dot_general x12, matrix products, contract_cols(): lax.dot_general(left_op, right_op, (((1,), (1,)), ((), ())), preferred_el...  81.4 us
  transfers between devices with their start and end apart: 27, of which 21 were waited for; matrix products, arithmetic and copies ran while one was open for 26% of the time, Pallas kernels for 0%

profile of v1, /device:TPU:0, one launch (start us, length us, event | category | flops | bytes accessed | tf_op | source)
XLA Modules:
  0.0 2374.3 jit_solution(8951440777238718284)
XLA Ops:
  12.7 44.1 %all-reduce.17 = (bf16[768]{0:T(1024)(128)(2,1)S(1)}, bf16[768]{0:T(1024)(128)(2,1)S(1)}) all-reduce(bf16[768]{0:T(1024)(128)(2,1)S(1)} %dynamic-update-slice, bf16[768]{0:T(1024)(128)(2,1)S(1)} %dynamic-update-slice.1), channel_id=2, replica_groups=mesh['section'=2,'dp'=4,'ctx'=4] {'dp','ctx'}, use_global_device_ids=true, to_apply=%add.12 | all-reduce | flops 1536 | bytes 6144
  62.2 23.0 all-gather.32.cloned.1.call-done
  85.3 5.9 copy.104
  109.1 106.4 %all-gather.26.cloned.1.call-done = bf16[4,1024,768]{1,2,0:T(8,128)(2,1)} async-done(((bf16[4,256,768]{1,2,0:T(8,128)(2,1)}), bf16[4,1024,768]{1,2,0:T(8,128)(2,1)}) %all-gather.26.cloned.1.call-update) | async-done | bytes 6291472 | tf_op jit(solution)/shard_map/all_gather | solution.py:9
  219.1 11.8 select_reduce_fusion.2
  230.9 10.9 exponential_reduce_fusion.2
  241.8 11.5 broadcast_select_fusion.2
  255.2 18.0 all-gather.34.cloned.1.call-done
  276.4 79.3 %all-gather.36.cloned.1.call-done = bf16[1,768,3072]{2,1,0:T(8,128)(2,1)} async-done(((bf16[1,48,3072]{2,1,0:T(8,128)(2,1)}), bf16[1,768,3072]{2,1,0:T(8,128)(2,1)}) %all-gather.36.cloned.1.call-update) | async-done | bytes 4718608 | tf_op jit(solution)/shard_map/all_gather | solution.py:135
  359.6 21.1 bitcast_dynamic-update-slice_fusion.5
  380.8 57.3 %all-gather.38.cloned.1.call-done = bf16[1,3072,768]{2,1,0:T(8,128)(2,1)} async-done(((bf16[1,192,768]{2,1,0:T(8,128)(2,1)}), bf16[1,3072,768]{2,1,0:T(8,128)(2,1)}) %all-gather.38.cloned.1.call-update) | async-done | bytes 4718608 | tf_op jit(solution)/shard_map/all_gather | solution.py:136
  438.0 7.1 fusion.400
  479.8 91.9 %all-gather.28.cloned.1.call-done = bf16[4,1024,768]{1,2,0:T(8,128)(2,1)} async-done(((bf16[4,256,768]{1,2,0:T(8,128)(2,1)}), bf16[4,1024,768]{1,2,0:T(8,128)(2,1)}) %all-gather.28.cloned.1.call-update) | async-done | bytes 6291472 | tf_op jit(solution)/shard_map/all_gather | solution.py:9
  575.4 12.2 select_reduce_fusion.1
  587.6 10.9 exponential_reduce_fusion.1
  598.5 10.6 fusion.215
  612.6 20.4 bitcast_dynamic-update-slice_fusion.4
  723.2 6.2 bitcast_dynamic-update-slice_fusion.1
  741.5 12.4 all-gather.40.cloned.1.call-done
  758.5 14.1 fusion.406
  772.6 45.0 %all-gather.42.cloned.1.call-done = bf16[1,2,1024,768]{3,2,1,0:T(8,128)(2,1)} async-done(((bf16[1,2,256,768]{3,2,1,0:T(8,128)(2,1)}), bf16[1,2,1024,768]{3,2,1,0:T(8,128)(2,1)}) %all-gather.42.cloned.1.call-update) | async-done | bytes 3145744 | tf_op jit(solution)/shard_map/all_gather | solution.py:279
  822.3 110.5 %all-gather.30.cloned.1.call-done = bf16[4,1024,768]{1,2,0:T(8,128)(2,1)} async-done(((bf16[4,256,768]{1,2,0:T(8,128)(2,1)}), bf16[4,1024,768]{1,2,0:T(8,128)(2,1)}) %all-gather.30.cloned.1.call-update) | async-done | bytes 6291472 | tf_op jit(solution)/shard_map/all_gather | solution.py:9
  936.4 11.8 select_reduce_fusion
  948.3 11.0 exponential_reduce_fusion
  959.3 10.9 fusion.214
  979.5 19.9 bitcast_dynamic-update-slice_fusion.3
  1004.0 20.0 fusion.43
  1037.5 17.0 multiply_reduce_fusion.2
  1054.4 16.7 multiply_convert_fusion.2
  1077.7 12.8 fusion.170
  1093.0 5.0 copy.134
  1098.4 9.5 bitcast_multiply_fusion.13
  1109.9 27.1 %reduce-scatter.11.cloned.1.call-done = bf16[2,256,768]{1,2,0:T(8,128)(2,1)} async-done(((bf16[2,1024,768]{1,2,0:T(8,128)(2,1)}), bf16[2,256,768]{1,2,0:T(8,128)(2,1)}) %reduce-scatter.11.cloned.1.call-update) | async-done | bytes 786448 | tf_op jit(solution)/shard_map/reduce_scatter | solution.py:284
  1139.8 59.7 %reduce-scatter.13.cloned.1.call-done = bf16[2,256,768]{1,2,0:T(8,128)(2,1)} async-done(((bf16[2,1024,768]{1,2,0:T(8,128)(2,1)}), bf16[2,256,768]{1,2,0:T(8,128)(2,1)}) %reduce-scatter.13.cloned.1.call-update) | async-done | bytes 786448 | tf_op jit(solution)/shard_map/reduce_scatter | solution.py:287
  1214.6 10.6 fusion.407
  1225.2 39.4 %all-gather.46.cloned.1.call-done = bf16[1,2,1024,768]{3,2,1,0:T(8,128)(2,1)} async-done(((bf16[1,2,256,768]{3,2,1,0:T(8,128)(2,1)}), bf16[1,2,1024,768]{3,2,1,0:T(8,128)(2,1)}) %all-gather.46.cloned.1.call-update) | async-done | bytes 3145744 | tf_op jit(solution)/shard_map/all_gather | solution.py:279
  1270.5 18.9 fusion.48
  1296.4 18.1 multiply_reduce_fusion.1
  1314.5 16.6 multiply_convert_fusion.1
  1336.7 12.8 fusion.173
  1355.4 10.6 bitcast_multiply_fusion.11
  1368.0 27.4 %reduce-scatter.15.cloned.1.call-done = bf16[2,256,768]{1,2,0:T(8,128)(2,1)} async-done(((bf16[2,1024,768]{1,2,0:T(8,128)(2,1)}), bf16[2,256,768]{1,2,0:T(8,128)(2,1)}) %reduce-scatter.15.cloned.1.call-update) | async-done | bytes 786448 | tf_op jit(solution)/shard_map/reduce_scatter | solution.py:284
  1398.2 59.7 %reduce-scatter.17.cloned.1.call-done = bf16[2,256,768]{1,2,0:T(8,128)(2,1)} async-done(((bf16[2,1024,768]{1,2,0:T(8,128)(2,1)}), bf16[2,256,768]{1,2,0:T(8,128)(2,1)}) %reduce-scatter.17.cloned.1.call-update) | async-done | bytes 786448 | tf_op jit(solution)/shard_map/reduce_scatter | solution.py:287
  1472.4 10.6 fusion.408
  1483.0 39.8 %all-gather.50.cloned.1.call-done = bf16[1,2,1024,768]{3,2,1,0:T(8,128)(2,1)} async-done(((bf16[1,2,256,768]{3,2,1,0:T(8,128)(2,1)}), bf16[1,2,1024,768]{3,2,1,0:T(8,128)(2,1)}) %all-gather.50.cloned.1.call-update) | async-done | bytes 3145744 | tf_op jit(solution)/shard_map/all_gather | solution.py:279
  1529.9 18.2 fusion.53
  1560.6 18.2 multiply_reduce_fusion
  1578.8 16.7 multiply_convert_fusion
  1601.1 13.1 fusion.176
  1636.4 4.9 fusion.263
  1641.3 5.3 fusion.264
  1646.6 8.9 select_add_fusion.1
  1661.4 4.7 fusion.163
  1666.1 9.1 select_add_fusion
  1677.2 7.0 fusion.256
  1684.3 5.2 fusion.259
  1689.5 8.6 bitcast_multiply_fusion.9
  1702.9 20.5 reduce-scatter.21.cloned.1.call-done
  1729.7 8.6 select_add_fusion.2
  1758.7 42.0 %all-reduce.16 = (f32[768]{0:T(1024)S(1)}, f32[768]{0:T(1024)S(1)}) all-reduce(f32[768]{0:T(1024)S(1)} %select_add_fusion.5, f32[768]{0:T(1024)S(1)} %select_add_fusion.4), channel_id=24, replica_groups=mesh['section'=2,'dp'=4,'ctx'=4] {'dp','ctx'}, use_global_device_ids=true, to_apply=%region_58.59.clone | all-reduce | flops 1536 | bytes 12288
  1807.1 49.3 %reduce-scatter.25.cloned.1.call-done = f32[48,768]{1,0:T(8,128)} async-done(((f32[768,768]{1,0:T(8,128)}), f32[48,768]{1,0:T(8,128)}) %reduce-scatter.25.cloned.1.call-update) | async-done | bytes 147472 | tf_op jit(solution)/shard_map/reduce_scatter | solution.py:336
  1856.4 177.4 %reduce-scatter.27.cloned.1.call-done = f32[48,3072]{1,0:T(8,128)} async-done(((f32[768,3072]{1,0:T(8,128)}), f32[48,3072]{1,0:T(8,128)}) %reduce-scatter.27.cloned.1.call-update) | async-done | bytes 589840 | tf_op jit(solution)/shard_map/reduce_scatter | solution.py:337
  2033.8 176.7 %reduce-scatter.29.cloned.1.call-done = f32[192,768]{1,0:T(8,128)} async-done(((f32[3072,768]{1,0:T(8,128)}), f32[192,768]{1,0:T(8,128)}) %reduce-scatter.29.cloned.1.call-update) | async-done | bytes 589840 | tf_op jit(solution)/shard_map/reduce_scatter | solution.py:338
  2210.5 157.1 %reduce-scatter.23.cloned.1.call-done = f32[48,2304]{1,0:T(8,128)} async-done(((f32[768,2304]{1,0:T(8,128)}), f32[48,2304]{1,0:T(8,128)}) %reduce-scatter.23.cloned.1.call-update) | async-done | bytes 442384 | tf_op jit(solution)/shard_map/reduce_scatter | solution.py:335
  (751 shorter events, 388.2 us)
Async XLA Ops:
  7.2 78.1 %all-gather.32.cloned.1.call-start = ((), (), s32[]{:S(2)}) async-start(), calls=%async_computation.23 | async-start | bytes 3760128 | tf_op jit(solution)/shard_map/all_gather | solution.py:133
  9.0 206.5 %all-gather.26.cloned.1.call-start = ((), (), s32[]{:S(2)}) async-start(), calls=%async_computation.10 | async-start | bytes 7864320 | tf_op jit(solution)/shard_map/all_gather | solution.py:9
  56.8 602.8 %copy-start.144 = (f32[768]{0:T(1024)}, f32[768]{0:T(1024)S(1)}, u32[]{:S(2)}) copy-start(f32[768]{0:T(1024)S(1)} %convert_element_type.771) | copy-start | bytes 9220
  59.1 516.3 %copy-start.63 = (f32[256,64]{0,1:T(8,128)}, f32[256,64]{0,1:T(8,128)S(1)}, u32[]{:S(2)}) copy-start(f32[256,64]{0,1:T(8,128)S(1)} %get-tuple-element.141) | copy-start | bytes 196612
  59.1 516.3 %copy-start.68 = (f32[256,64]{0,1:T(8,128)}, f32[256,64]{0,1:T(8,128)S(1)}, u32[]{:S(2)}) copy-start(f32[256,64]{0,1:T(8,128)S(1)} %get-tuple-element.140) | copy-start | bytes 196612
  99.3 358.3 %copy-start.23 = (f32[256,12,64]{0,2,1:T(8,128)}, f32[256,12,64]{0,2,1:T(8,128)S(1)}, u32[]{:S(2)}) copy-start(f32[256,12,64]{0,2,1:T(8,128)S(1)} %mul.972) | copy-start | bytes 2359300
  99.4 355.4 %copy-start.25 = (f32[256,12,64]{0,2,1:T(8,128)}, f32[256,12,64]{0,2,1:T(8,128)S(1)}, u32[]{:S(2)}) copy-start(f32[256,12,64]{0,2,1:T(8,128)S(1)} %mul.968) | copy-start | bytes 2359300
  101.9 171.3 %all-gather.34.cloned.1.call-start = ((), (), s32[]{:S(2)}) async-start(), calls=%async_computation.24 | async-start | bytes 1253376 | tf_op jit(solution)/shard_map/all_gather | solution.py:134
  102.7 253.1 %all-gather.36.cloned.1.call-start = ((), (), s32[]{:S(2)}) async-start(), calls=%async_computation.25 | async-start | bytes 5013504 | tf_op jit(solution)/shard_map/all_gather | solution.py:135
  104.6 333.5 %all-gather.38.cloned.1.call-start = ((), (), s32[]{:S(2)}) async-start(), calls=%async_computation.26 | async-start | bytes 5013504 | tf_op jit(solution)/shard_map/all_gather | solution.py:136
  106.4 465.3 %all-gather.28.cloned.1.call-start = ((), (), s32[]{:S(2)}) async-start(), calls=%async_computation.11 | async-start | bytes 7864320 | tf_op jit(solution)/shard_map/all_gather | solution.py:9
  107.4 920.3 %copy-start.131 = (f32[768]{0:T(1024)}, f32[768]{0:T(1024)S(1)}, u32[]{:S(2)}) copy-start(f32[768]{0:T(1024)S(1)} %convert_element_type.772) | copy-start | bytes 9220
  109.1 110.0 %copy-start.79 = (f32[2,256,12,32]{1,3,2,0:T(8,128)}, f32[2,256,12,32]{1,3,2,0:T(8,128)S(1)}, u32[]{:S(2)}) copy-start(f32[2,256,12,32]{1,3,2,0:T(8,128)S(1)} %get-tuple-element.131) | copy-start | bytes 2359300
  109.1 110.0 %copy-start.80 = (f32[2,256,12,32]{1,3,2,0:T(8,128)}, f32[2,256,12,32]{1,3,2,0:T(8,128)S(1)}, u32[]{:S(2)}) copy-start(f32[2,256,12,32]{1,3,2,0:T(8,128)S(1)} %get-tuple-element.132) | copy-start | bytes 2359300
  276.1 161.9 %copy-start.33 = (f32[512,768]{1,0:T(8,128)}, f32[512,768]{1,0:T(8,128)S(1)}, u32[]{:S(2)}) copy-start(f32[512,768]{1,0:T(8,128)S(1)} %get-tuple-element.153) | copy-start | bytes 4718596
  445.2 3.4 collective-permute-start
  448.9 161.3 %copy-start.19 = (f32[2,256,768]{2,1,0:T(8,128)}, f32[2,256,768]{2,1,0:T(8,128)S(1)}, u32[]{:S(2)}) copy-start(f32[2,256,768]{2,1,0:T(8,128)S(1)} %get-tuple-element.69) | copy-start | bytes 4718596
  457.6 296.3 %all-gather.40.cloned.1.call-start = ((), (), s32[]{:S(2)}) async-start(), calls=%async_computation.27 | async-start | bytes 3932160 | tf_op jit(solution)/shard_map/all_gather | solution.py:278
  610.7 22.3 slice-start.7
  611.7 21.4 copy-start.40
  612.6 20.5 slice-start.8
  637.1 20.5 collective-permute-start.1
  692.0 125.6 %all-gather.42.cloned.1.call-start = ((), (), s32[]{:S(2)}) async-start(), calls=%async_computation.28 | async-start | bytes 3932160 | tf_op jit(solution)/shard_map/all_gather | solution.py:279
  699.4 233.3 %all-gather.30.cloned.1.call-start = ((), (), s32[]{:S(2)}) async-start(), calls=%async_computation.12 | async-start | bytes 7864320 | tf_op jit(solution)/shard_map/all_gather | solution.py:9
  703.7 389.3 %all-gather.44.cloned.1.call-start = ((), (), s32[]{:S(2)}) async-start(), calls=%async_computation.29 | async-start | bytes 3932160 | tf_op jit(solution)/shard_map/all_gather | solution.py:278
  741.0 396.0 %reduce-scatter.11.cloned.1.call-start = ((), (), s32[]{:S(2)}) async-start(), calls=%async_computation.13 | async-start | bytes 3932160 | tf_op jit(solution)/shard_map/reduce_scatter | solution.py:284
  822.3 114.1 %copy-start.64 = (f32[256,64]{0,1:T(8,128)S(1)}, f32[256,64]{0,1:T(8,128)}, u32[]{:S(2)}) copy-start(f32[256,64]{0,1:T(8,128)} %copy-done.63) | copy-start | bytes 196612
  822.3 114.1 %copy-start.69 = (f32[256,64]{0,1:T(8,128)S(1)}, f32[256,64]{0,1:T(8,128)}, u32[]{:S(2)}) copy-start(f32[256,64]{0,1:T(8,128)} %copy-done.68) | copy-start | bytes 196612
  975.8 23.6 slice-start
  977.4 21.9 copy-start.152
  977.7 21.6 copy-start.175
  999.4 24.5 %slice-start.11 = ((s8[4718592]{0:T(1024)(128)(4,1)}), s8[4194304]{0:T(1024)(128)(4,1)S(1)}, s32[]{:S(2)}) async-start(s8[4718592]{0:T(1024)(128)(4,1)} %bitcast.959), calls=%async_computation.44 | async-start | bytes 8388608
  1003.9 20.0 copy-start.4
  1003.9 20.0 copy-start.153
  1076.6 122.9 %reduce-scatter.13.cloned.1.call-start = ((), (), s32[]{:S(2)}) async-start(), calls=%async_computation.14 | async-start | bytes 3932160 | tf_op jit(solution)/shard_map/reduce_scatter | solution.py:287
  1090.5 174.1 %all-gather.46.cloned.1.call-start = ((), (), s32[]{:S(2)}) async-start(), calls=%async_computation.30 | async-start | bytes 3932160 | tf_op jit(solution)/shard_map/all_gather | solution.py:279
  1091.3 260.7 %all-gather.48.cloned.1.call-start = ((), (), s32[]{:S(2)}) async-start(), calls=%async_computation.31 | async-start | bytes 3932160 | tf_op jit(solution)/shard_map/all_gather | solution.py:278
  1092.9 302.5 %reduce-scatter.15.cloned.1.call-start = ((), (), s32[]{:S(2)}) async-start(), calls=%async_computation.15 | async-start | bytes 3932160 | tf_op jit(solution)/shard_map/reduce_scatter | solution.py:284
  1098.0 112.1 %copy-start.162 = (f32[512]{0:T(512)}, f32[512]{0:T(512)S(1)}, u32[]{:S(2)}) copy-start(f32[512]{0:T(512)S(1)} %broadcast_multiply_fusion.7) | copy-start | bytes 6148
  1098.3 111.7 %copy-start.164 = (f32[512]{0:T(512)}, f32[512]{0:T(512)S(1)}, u32[]{:S(2)}) copy-start(f32[512]{0:T(512)S(1)} %fusion.347) | copy-start | bytes 6148
  1098.3 106.0 %copy-start.171 = (f32[512]{0:T(512)}, f32[512]{0:T(512)S(1)}, u32[]{:S(2)}) copy-start(f32[512]{0:T(512)S(1)} %broadcast_multiply_fusion.3) | copy-start | bytes 6148
  1098.4 106.0 %copy-start.166 = (f32[512]{0:T(512)}, f32[512]{0:T(512)S(1)}, u32[]{:S(2)}) copy-start(f32[512]{0:T(512)S(1)} %broadcast_multiply_fusion.5) | copy-start | bytes 6148
  1107.9 29.1 %copy-start.70 = (f32[256,64]{0,1:T(8,128)S(1)}, f32[256,64]{0,1:T(8,128)}, u32[]{:S(2)}) copy-start(f32[256,64]{0,1:T(8,128)} %copy-done.68) | copy-start | bytes 196612
  1109.9 28.7 %copy-start.65 = (f32[256,64]{0,1:T(8,128)S(1)}, f32[256,64]{0,1:T(8,128)}, u32[]{:S(2)}) copy-start(f32[256,64]{0,1:T(8,128)} %copy-done.63) | copy-start | bytes 196612
  1213.3 56.0 %collective-permute-start.2 = (bf16[2,256,768]{2,1,0:T(8,128)(2,1)}, bf16[2,256,768]{2,1,0:T(8,128)(2,1)S(1)}, u32[]{:S(2)}, u32[]{:S(2)}) collective-permute-start(bf16[2,256,768]{2,1,0:T(8,128)(2,1)} %bitcast.112), channel_id=1, source_target_pairs={{16,0},{17,1},{18,2},{19,3},{20,4},{21,5},{22,6},{23,7},{24,8},{25... | collective-permute-start | bytes 2359304 | tf_op jit(solution)/shard_map/ppermute | solution.py:18
  1225.2 44.1 %copy-start.107 = (bf16[2,2,256,768]{3,2,1,0:T(8,128)(2,1)S(1)}, bf16[2,2,256,768]{3,2,1,0:T(8,128)(2,1)}, u32[]{:S(2)}) copy-start(bf16[2,2,256,768]{3,2,1,0:T(8,128)(2,1)} %param.10) | copy-start | bytes 4718596
  1269.3 23.7 copy-start.160
  1269.3 20.2 slice-start.13
  1336.7 121.2 %reduce-scatter.17.cloned.1.call-start = ((), (), s32[]{:S(2)}) async-start(), calls=%async_computation.16 | async-start | bytes 3932160 | tf_op jit(solution)/shard_map/reduce_scatter | solution.py:287
  1349.5 173.2 %all-gather.50.cloned.1.call-start = ((), (), s32[]{:S(2)}) async-start(), calls=%async_computation.32 | async-start | bytes 3932160 | tf_op jit(solution)/shard_map/all_gather | solution.py:279
  1351.9 348.2 %reduce-scatter.19.cloned.1.call-start = ((), (), s32[]{:S(2)}) async-start(), calls=%async_computation.17 | async-start | bytes 3932160 | tf_op jit(solution)/shard_map/reduce_scatter | solution.py:284
  1355.4 117.0 %copy-start.14 = (bf16[1,2,1024,768]{2,3,1,0:T(8,128)(2,1)}, bf16[1,2,1024,768]{2,3,1,0:T(8,128)(2,1)S(1)}, u32[]{:S(2)}) copy-start(bf16[1,2,1024,768]{2,3,1,0:T(8,128)(2,1)S(1)} %copy.141) | copy-start | bytes 9437188
  1355.4 112.5 %copy-start.169 = (f32[512]{0:T(512)}, f32[512]{0:T(512)S(1)}, u32[]{:S(2)}) copy-start(f32[512]{0:T(512)S(1)} %fusion.349) | copy-start | bytes 6148
  1366.0 29.4 %copy-start.71 = (f32[256,64]{0,1:T(8,128)S(1)}, f32[256,64]{0,1:T(8,128)}, u32[]{:S(2)}) copy-start(f32[256,64]{0,1:T(8,128)} %copy-done.68) | copy-start | bytes 196612
  1368.0 29.0 %copy-start.66 = (f32[256,64]{0,1:T(8,128)S(1)}, f32[256,64]{0,1:T(8,128)}, u32[]{:S(2)}) copy-start(f32[256,64]{0,1:T(8,128)} %copy-done.63) | copy-start | bytes 196612
  1471.1 56.3 %collective-permute-start.3 = (bf16[2,256,768]{2,1,0:T(8,128)(2,1)}, bf16[2,256,768]{2,1,0:T(8,128)(2,1)}, u32[]{:S(2)}, u32[]{:S(2)}) collective-permute-start(bf16[2,256,768]{2,1,0:T(8,128)(2,1)} %bitcast.136), channel_id=1, source_target_pairs={{16,0},{17,1},{18,2},{19,3},{20,4},{21,5},{22,6},{23,7},{24,8},{25... | collective-permute-start | bytes 2359304 | tf_op jit(solution)/shard_map/ppermute | solution.py:18
  1483.0 44.4 %copy-start.179 = (f32[512]{0:T(512)S(1)}, f32[512]{0:T(512)}, u32[]{:S(2)}) copy-start(f32[512]{0:T(512)} %get-tuple-element.20) | copy-start | bytes 6148
  1483.0 44.4 %copy-start.108 = (bf16[2,2,256,768]{3,2,1,0:T(8,128)(2,1)S(1)}, bf16[2,2,256,768]{3,2,1,0:T(8,128)(2,1)}, u32[]{:S(2)}) copy-start(bf16[2,2,256,768]{3,2,1,0:T(8,128)(2,1)} %param.10) | copy-start | bytes 4718596
  1527.4 20.7 slice-start.15
  1601.0 122.3 %reduce-scatter.21.cloned.1.call-start = ((), (), s32[]{:S(2)}) async-start(), calls=%async_computation.18 | async-start | bytes 3932160 | tf_op jit(solution)/shard_map/reduce_scatter | solution.py:287
  1614.2 242.2 %reduce-scatter.25.cloned.1.call-start = ((), (), s32[]{:S(2)}) async-start(), calls=%async_computation.20 | async-start | bytes 2506752 | tf_op jit(solution)/shard_map/reduce_scatter | solution.py:336
  1636.3 397.5 %reduce-scatter.27.cloned.1.call-start = ((), (), s32[]{:S(2)}) async-start(), calls=%async_computation.21 | async-start | bytes 10027008 | tf_op jit(solution)/shard_map/reduce_scatter | solution.py:337
  1655.6 554.9 %reduce-scatter.29.cloned.1.call-start = ((), (), s32[]{:S(2)}) async-start(), calls=%async_computation.22 | async-start | bytes 10027008 | tf_op jit(solution)/shard_map/reduce_scatter | solution.py:338
  1675.3 692.2 %reduce-scatter.23.cloned.1.call-start = ((), (), s32[]{:S(2)}) async-start(), calls=%async_computation.19 | async-start | bytes 7520256 | tf_op jit(solution)/shard_map/reduce_scatter | solution.py:335
  (175 other events, 836.3 us)
Sparse Core Ops, SparseCore 0:
  11.3 73.9 all-gather.31
  102.1 113.3 all-gather.25
  218.8 54.3 all-gather.33
  276.4 79.3 all-gather.35
  358.9 79.0 all-gather.37
  457.7 113.9 all-gather.27
  692.1 61.6 all-gather.39
  755.4 62.1 all-gather.41
  819.2 113.5 all-gather.29
  934.1 61.6 all-gather.43
  1076.7 60.2 reduce-scatter.10
  1139.2 60.2 reduce-scatter.12
  1201.1 63.4 all-gather.45
  1266.0 62.1 all-gather.47
  1336.8 58.5 reduce-scatter.14
  1397.6 60.2 reduce-scatter.16
  1459.3 63.4 all-gather.49
  1601.1 58.9 reduce-scatter.18
  1663.0 60.2 reduce-scatter.20
  1728.7 127.6 reduce-scatter.24
  1863.6 170.1 reduce-scatter.26
  2040.1 170.3 reduce-scatter.28
  2217.3 150.2 reduce-scatter.22
